TPU v7x, 512 devices: a whole 4x8x8 slice. The times are simulated.
512 devices in a mesh: row: 32 (over y, x_hi, core), col: 16 (over z, x_lo).
Axes of the slice: x: 4 (x_hi: 2, x_lo: 2; x = x_hi * 2 + x_lo), y: 8, z: 8, core: 2. Of those that a mesh axis runs over, the one named last changes fastest.
Arguments:
- temps: bfloat16 [12, 64, 262144], P(None, None, ('row', 'col')), may hold values from -6 to 6
- sensors: int32 [12, 2048], replicated, may hold values from 0 to 262143
Outputs:
- corr: bfloat16 [2048, 262144], P('col', 'row')
Inputs may be any that keep to these rules, and one draw needn't show every extreme that they name: `sensors`: each entry is a pixel index of its tier; candidates may repeat.
All inputs are finite; a program needn't handle non-finite values.
Results may differ from a plain program's by a relative error of at most 0.001.
Values may be sent and summed in bfloat16 or wider, within the bound.
No kernel may reach another device: no remote copies, remote signals or barrier semaphores. Data moves between devices by JAX's collectives and lax.ppermute only.
A program may use at most 64 MiB of HBM per device.

v0:
```python
import jax
import jax.numpy as jnp
from jax import lax
from jax.sharding import Mesh
from jax.sharding import PartitionSpec as P

COL = ("col_0", "col_1")
ROW_COL = ("row", "col_0", "col_1")


def scatter_axes(value, axes, dim):
    for axis in axes:
        value = lax.psum_scatter(value, axis, scatter_dimension=dim, tiled=True)
    return value


def filled_up(lines, length):
    spare = -lines.shape[0] % length
    if not spare:
        return lines
    return jnp.concatenate([lines, jnp.zeros((spare, *lines.shape[1:]), lines.dtype)])


def sent_to_all(value, axis):
    length = lax.axis_size(axis)
    return lax.all_to_all(
        jnp.broadcast_to(value[None], (length, *value.shape)), axis, 0, 0, tiled=True
    )


def laid_out(blocks, dim):
    blocks = jnp.moveaxis(blocks, 0, dim)
    shape = blocks.shape
    return blocks.reshape(*shape[:dim], shape[dim] * shape[dim + 1], *shape[dim + 2 :])


def gather_directly(value, axis, dim):
    blocks = sent_to_all(value, axis)
    return laid_out(blocks, dim)


def in_blocks(value, dim, length):
    before, after = (value.shape[:dim], value.shape[dim + 1 :])
    return jnp.moveaxis(value.reshape(*before, length, -1, *after), dim, 0)


def sent_and_summed(value, axis, dim):
    blocks = in_blocks(value, dim, lax.axis_size(axis))
    arrived = lax.all_to_all(blocks, axis, split_axis=0, concat_axis=0, tiled=True)
    return arrived.astype(jnp.float32).sum(axis=0)


def total_of(value, axes):
    lines = value.reshape(-1, value.shape[-1])
    padded = filled_up(lines, lax.axis_size(axes))
    whole = gather_directly(sent_and_summed(padded, axes, 0).astype(jnp.bfloat16), axes, 0)
    return lax.slice_in_dim(whole, 0, len(lines)).reshape(value.shape).astype(jnp.float32)


def select_columns(fields, sensor_rows, first_pixel):
    width = fields.shape[2]
    offsets = sensor_rows - first_pixel
    pixel_ids = lax.broadcasted_iota(jnp.int32, (width, sensor_rows.shape[1]), 0)

    def one_tier(pair):
        tier_fields, tier_offsets = pair
        selector = (pixel_ids == tier_offsets[None, :]).astype(jnp.bfloat16)
        return jnp.dot(tier_fields, selector, preferred_element_type=jnp.float32)

    return lax.map(one_tier, (fields, offsets))


def body(temps, sensors):
    col_count = lax.axis_size(COL)
    first_pixel = (lax.axis_index("row") * col_count + lax.axis_index(COL)) * temps.shape[2]
    local_values = select_columns(temps, sensors, first_pixel)
    owned = (
        scatter_axes(local_values.astype(jnp.bfloat16), COL, 2)
        .astype(jnp.float32)
        .astype(jnp.bfloat16)
    )
    readings = total_of(owned, "row").astype(jnp.bfloat16)
    scale_factor = 1.0 / jnp.sqrt(jnp.float32(temps.shape[0] * temps.shape[1]))
    summed = jnp.einsum(
        "tsc,tsp->cp",
        lax.all_gather(readings, COL, axis=2, tiled=True),
        temps,
        preferred_element_type=jnp.float32,
    )
    rounded = (summed * scale_factor).astype(jnp.bfloat16)
    return lax.all_to_all(rounded, COL, split_axis=0, concat_axis=1, tiled=True)


def solution(mesh):
    torus = Mesh(mesh.devices.reshape(mesh.shape["row"], 8, 2), ("row", "col_0", "col_1"))
    in_specs = (P(None, None, ROW_COL), P())
    out_specs = P(COL, "row")
    return jax.shard_map(body, mesh=torus, in_specs=in_specs, out_specs=out_specs, check_vma=False)
```

profile of v0, /device:TPU:4, one launch (start us, length us, event | category | flops | bytes accessed | tf_op | source)
XLA Modules:
  0.0 315.9 jit_solution(11540507424467396206)
XLA Ops:
  7.5 29.6 %while.11 = (s32[]{:T(128)}, bf16[12,64,2048]{2,1,0:T(8,128)(2,1)}, bf16[12,64,512]{2,1,0:T(8,128)(2,1)}, s32[12,2048]{1,0:T(8,128)S(1)}, s32[]{:T(128)}) while((s32[]{:T(128)}, bf16[12,64,2048]{2,1,0:T(8,128)(2,1)}, bf16[12,64,512]{2,1,0:T(8,128)(2,1)}, s32[12,2048]{1,0:T(8,128)S(1)}, s32[]{:T(128)}) %tuple.21), condition=%wide.region_1.2_spmd.clone, body=%wide.region_0.1_spmd.clone.sunk | while | flops 135266304 | bytes 615489 | solution.py:70
  7.5 2.4 fusion.15
  9.9 2.5 fusion.15
  12.4 2.4 fusion.15
  14.9 2.5 fusion.15
  17.3 2.5 fusion.15
  19.8 2.5 fusion.15
  22.3 2.5 fusion.15
  24.7 2.4 fusion.15
  27.2 2.5 fusion.15
  29.7 2.5 fusion.15
  32.2 2.5 fusion.15
  34.6 2.5 fusion.15
  37.2 54.7 %reduce-scatter.5.cloned.1.call-done = bf16[12,64,256]{2,1,0:T(8,128)(2,1)} async-done(((bf16[12,64,2048]{2,1,0:T(8,128)(2,1)}), bf16[12,64,256]{2,1,0:T(8,128)(2,1)}) %reduce-scatter.5.cloned.1.call-update) | async-done | bytes 393232 | tf_op jit(solution)/shard_map/reduce_scatter | solution.py:13
  91.9 1.9 copy.5
  93.8 1.4 reshape.5
  95.3 19.6 %reduce-scatter.7.cloned.1.call-done = bf16[128,768]{1,0:T(8,128)(2,1)} async-done(((bf16[256,768]{1,0:T(8,128)(2,1)}), bf16[128,768]{1,0:T(8,128)(2,1)}) %reduce-scatter.7.cloned.1.call-update) | async-done | bytes 196624
  114.9 1.3 reshape.6
  116.6 20.3 %all_to_all.29 = bf16[32,24,128]{2,1,0:T(8,128)(2,1)S(1)} all-to-all(bf16[32,24,128]{2,1,0:T(8,128)(2,1)S(1)} %bitcast.33), channel_id=1, replica_groups=mesh['row'=32,'col_0'=8,'col_1'=2] {'row'}, dimensions={0} | all-to-all | bytes 393216 | tf_op jit(solution)/shard_map/all_to_all | solution.py:49
  137.0 15.6 %all_to_all.30 = bf16[32,24,128]{2,1,0:T(8,128)(2,1)} all-to-all(bf16[32,24,128]{2,1,0:T(8,128)(2,1)S(1)} %broadcast_in_dim.15), channel_id=1, replica_groups=mesh['row'=32,'col_0'=8,'col_1'=2] {'row'}, dimensions={0} | all-to-all | bytes 393216 | tf_op jit(solution)/shard_map/all_to_all | solution.py:26
  152.6 99.3 %all-gather.2.cloned.1.call-done = bf16[12,64,2048]{2,1,0:T(8,128)(2,1)} async-done(((bf16[12,64,128]{2,1,0:T(8,128)(2,1)}), bf16[12,64,2048]{2,1,0:T(8,128)(2,1)}) %all-gather.2.cloned.1.call-update) | async-done | bytes 3145744 | tf_op jit(solution)/shard_map/all_gather | solution.py:86
  251.9 3.7 %fusion.9 = bf16[2048,512]{1,0:T(8,128)(2,1)S(1)} fusion(bf16[12,64,2048]{2,1,0:T(8,128)(2,1)} %all-gather.2.cloned.1.call-done, bf16[12,64,512]{2,1,0:T(8,128)(2,1)S(1)} %copy-done), kind=kOutput, calls=%fused_computation.11 | convolution fusion | flops 1612709888 | bytes 6029312 | tf_op jit(solution)/shard_map/tsc,tsp->cp/dot_general | solution.py:84
  255.7 52.2 %all_to_all.31 = bf16[16,128,512]{2,1,0:T(8,128)(2,1)S(1)} all-to-all(bf16[16,128,512]{2,1,0:T(8,128)(2,1)S(1)} %bitcast.30), channel_id=1, replica_groups=mesh['row'=32,'col_0'=8,'col_1'=2] {'col_0','col_1'}, dimensions={0} | all-to-all | bytes 4194304 | tf_op jit(solution)/shard_map/all_to_all | solution.py:91
  307.9 1.5 copy.7
  (25 shorter events, 1.6 us)
Async XLA Ops:
  6.5 85.4 %reduce-scatter.5.cloned.1.call-start = ((), (), s32[]{:S(2)}) async-start(), calls=%async_computation.5 | async-start | bytes 3538944 | tf_op jit(solution)/shard_map/reduce_scatter | solution.py:13
  37.1 214.8 %copy-start = (bf16[12,64,512]{2,1,0:T(8,128)(2,1)S(1)}, bf16[12,64,512]{2,1,0:T(8,128)(2,1)}, u32[]{:S(2)}) copy-start(bf16[12,64,512]{2,1,0:T(8,128)(2,1)} %get-tuple-element.103) | copy-start | bytes 2359300
  37.1 77.8 %reduce-scatter.7.cloned.1.call-start = ((), (), s32[]{:S(2)}) async-start(), calls=%async_computation.7 | async-start | bytes 589824
  95.2 156.7 %all-gather.2.cloned.1.call-start = ((), (), s32[]{:S(2)}) async-start(), calls=%async_computation.6 | async-start | bytes 3342336 | tf_op jit(solution)/shard_map/all_gather | solution.py:86
Sparse Core Ops, SparseCore 0:
  37.2 54.6 reduce-scatter.4
  95.4 19.4 reduce-scatter.6
  152.8 99.1 all-gather.1
where the time goes:
time: 317 us; the launch traced here: 316 us
  waiting for transfers between devices  174 us (55%)
  blocking collectives  88.2 us (28%)
  matrix products  33.2 us (10%)
  between operations  13.2 us (4%)
  local copies, waits for them, and re-layouts  6.65 us (2%)
    all_gather x1, waiting for transfers between devices, body(): lax.all_gather(readings, COL, axis=2, tiled=True)  99.3 us
    reduce_scatter x1, waiting for transfers between devices, scatter_axes(): value = lax.psum_scatter(value, axis, scatter_dimension=dim, tiled=True)  54.7 us
    all_to_all x1, blocking collectives, body(): return lax.all_to_all(rounded, COL, split_axis=0, concat_axis=1, tiled=True)  52.2 us
    dot_general x12, matrix products, one_tier(): return jnp.dot(tier_fields, selector, preferred_element_type=jnp.float32)  29.5 us
    all_to_all x1, blocking collectives, sent_and_summed(): lax.all_to_all(blocks, axis, split_axis=0, concat_axis=0, tiled=True)  20.3 us
    unnamed x4, waiting for transfers between devices  19.7 us
    all_to_all x1, blocking collectives, sent_to_all(): lax.all_to_all(jnp.broadcast_to(value[None], (length, *value.shape)), axi...  15.6 us
  transfers between devices with their start and end apart: 3, of which 3 were waited for; matrix products, arithmetic and copies ran while one was open for 0% of the time, Pallas kernels for 0%

commit v1 on v0

--- a/solution.py
+++ b/solution.py
@@ -1,11 +1,23 @@
+import functools
 import jax
 import jax.numpy as jnp
 from jax import lax
 from jax.sharding import Mesh
 from jax.sharding import PartitionSpec as P
+from jax.lax import all_to_all, psum
 
 COL = ("col_0", "col_1")
 ROW_COL = ("row", "col_0", "col_1")
+
+
+def sheet_read(own_rows, bus_axis):
+    v_now = psum(1, bus_axis)
+    arr_now = jnp.stack(v_now * [own_rows])
+    z2 = all_to_all(arr_now, bus_axis, 0, 0)
+    return jnp.concatenate(z2, axis=2)
+
+
+produce_vectors = functools.partial(sheet_read, bus_axis=COL)
 
 
 def scatter_axes(value, axes, dim):
@@ -82,10 +94,7 @@
     readings = total_of(owned, "row").astype(jnp.bfloat16)
     scale_factor = 1.0 / jnp.sqrt(jnp.float32(temps.shape[0] * temps.shape[1]))
     summed = jnp.einsum(
-        "tsc,tsp->cp",
-        lax.all_gather(readings, COL, axis=2, tiled=True),
-        temps,
-        preferred_element_type=jnp.float32,
+        "tsc,tsp->cp", produce_vectors(readings), temps, preferred_element_type=jnp.float32
     )
     rounded = (summed * scale_factor).astype(jnp.bfloat16)
     return lax.all_to_all(rounded, COL, split_axis=0, concat_axis=1, tiled=True)

time: 317 us -> 300 us (0.946)
  the two profiles are of different devices: /device:TPU:4 before, /device:TPU:16 now
where the time goes in v1:
time: 300 us; the launch traced here: 299 us
  blocking collectives  171 us (57%)
  waiting for transfers between devices  74.6 us (25%)
  matrix products  31.4 us (10%)
  between operations  13.5 us (4%)
  local copies, waits for them, and re-layouts  7.43 us (2%)
    all_to_all x1, blocking collectives, sheet_read(): z2 = all_to_all(arr_now, bus_axis, 0, 0)  81 us
    reduce_scatter x1, waiting for transfers between devices, scatter_axes(): value = lax.psum_scatter(value, axis, scatter_dimension=dim, tiled=True)  54.7 us
    all_to_all x1, blocking collectives, body(): return lax.all_to_all(rounded, COL, split_axis=0, concat_axis=1, tiled=True)  54.2 us
    dot_general x12, matrix products, one_tier(): return jnp.dot(tier_fields, selector, preferred_element_type=jnp.float32)  29.5 us
    all_to_all x1, blocking collectives, sent_and_summed(): lax.all_to_all(blocks, axis, split_axis=0, concat_axis=0, tiled=True)  20.3 us
    unnamed x3, waiting for transfers between devices  19.9 us
    all_to_all x1, blocking collectives, sent_to_all(): lax.all_to_all(jnp.broadcast_to(value[None], (length, *value.shape)), axi...  15.5 us
  transfers between devices with their start and end apart: 2, of which 2 were waited for; matrix products, arithmetic and copies ran while one was open for 0% of the time, Pallas kernels for 0%

profile of v1, /device:TPU:16, one launch (start us, length us, event | category | flops | bytes accessed | tf_op | source)
XLA Modules:
  0.0 298.8 jit_solution(1203254065565712150)
XLA Ops:
  7.5 29.7 %while.11 = (s32[]{:T(128)}, bf16[12,64,2048]{2,1,0:T(8,128)(2,1)}, bf16[12,64,512]{2,1,0:T(8,128)(2,1)}, s32[12,2048]{1,0:T(8,128)S(1)}, s32[]{:T(128)}) while((s32[]{:T(128)}, bf16[12,64,2048]{2,1,0:T(8,128)(2,1)}, bf16[12,64,512]{2,1,0:T(8,128)(2,1)}, s32[12,2048]{1,0:T(8,128)S(1)}, s32[]{:T(128)}) %tuple.21), condition=%wide.region_1.2_spmd.clone, body=%wide.region_0.1_spmd.clone.sunk | while | flops 135266304 | bytes 615489 | solution.py:82
  7.5 2.4 fusion.17
  9.9 2.4 fusion.17
  12.4 2.5 fusion.17
  14.9 2.5 fusion.17
  17.4 2.5 fusion.17
  19.8 2.5 fusion.17
  22.3 2.5 fusion.17
  24.8 2.5 fusion.17
  27.3 2.5 fusion.17
  29.8 2.5 fusion.17
  32.2 2.5 fusion.17
  34.7 2.5 fusion.17
  37.2 54.7 %reduce-scatter.5.cloned.1.call-done = bf16[12,64,256]{2,1,0:T(8,128)(2,1)} async-done(((bf16[12,64,2048]{2,1,0:T(8,128)(2,1)}), bf16[12,64,256]{2,1,0:T(8,128)(2,1)}) %reduce-scatter.5.cloned.1.call-update) | async-done | bytes 393232 | tf_op jit(solution)/shard_map/reduce_scatter | solution.py:25
  91.9 1.9 copy.6
  93.9 1.4 reshape.16
  95.3 19.8 %reduce-scatter.7.cloned.1.call-done = bf16[128,768]{1,0:T(8,128)(2,1)} async-done(((bf16[256,768]{1,0:T(8,128)(2,1)}), bf16[128,768]{1,0:T(8,128)(2,1)}) %reduce-scatter.7.cloned.1.call-update) | async-done | bytes 196624
  115.1 1.3 reshape.17
  116.7 20.3 %all_to_all.34 = bf16[32,24,128]{2,1,0:T(8,128)(2,1)S(1)} all-to-all(bf16[32,24,128]{2,1,0:T(8,128)(2,1)S(1)} %bitcast.40), channel_id=1, replica_groups=mesh['row'=32,'col_0'=8,'col_1'=2] {'row'}, dimensions={0} | all-to-all | bytes 393216 | tf_op jit(solution)/shard_map/all_to_all | solution.py:61
  137.1 15.5 %all_to_all.35 = bf16[32,24,128]{2,1,0:T(8,128)(2,1)S(1)} all-to-all(bf16[32,24,128]{2,1,0:T(8,128)(2,1)S(1)} %broadcast_in_dim.15), channel_id=1, replica_groups=mesh['row'=32,'col_0'=8,'col_1'=2] {'row'}, dimensions={0} | all-to-all | bytes 393216 | tf_op jit(solution)/shard_map/all_to_all | solution.py:38
  153.4 81.0 %all_to_all.36 = bf16[16,12,64,128]{3,2,1,0:T(8,128)(2,1)S(1)} all-to-all(bf16[16,12,64,128]{3,2,1,0:T(8,128)(2,1)S(1)} %stack.5), channel_id=1, replica_groups=mesh['row'=32,'col_0'=8,'col_1'=2] {'col_0','col_1'}, dimensions={0} | all-to-all | bytes 6291456 | tf_op jit(solution)/shard_map/all_to_all | solution.py:16
  234.4 1.8 fusion.9
  236.2 54.2 %all_to_all.37 = bf16[16,128,512]{2,1,0:T(8,128)(2,1)S(1)} all-to-all(bf16[16,128,512]{2,1,0:T(8,128)(2,1)S(1)} %bitcast.37), channel_id=1, replica_groups=mesh['row'=32,'col_0'=8,'col_1'=2] {'col_0','col_1'}, dimensions={0} | all-to-all | bytes 4194304 | tf_op jit(solution)/shard_map/all_to_all | solution.py:100
  290.4 1.5 copy.9
  (24 shorter events, 2.4 us)
Async XLA Ops:
  6.5 85.4 %reduce-scatter.5.cloned.1.call-start = ((), (), s32[]{:S(2)}) async-start(), calls=%async_computation.6 | async-start | bytes 3538944 | tf_op jit(solution)/shard_map/reduce_scatter | solution.py:25
  37.2 77.9 %reduce-scatter.7.cloned.1.call-start = ((), (), s32[]{:S(2)}) async-start(), calls=%async_computation.7 | async-start | bytes 589824
  153.4 81.0 %copy-start = (bf16[12,64,512]{2,1,0:T(8,128)(2,1)S(1)}, bf16[12,64,512]{2,1,0:T(8,128)(2,1)}, u32[]{:S(2)}) copy-start(bf16[12,64,512]{2,1,0:T(8,128)(2,1)} %get-tuple-element.99) | copy-start | bytes 2359300
Sparse Core Ops, SparseCore 0:
  37.3 54.5 reduce-scatter.4
  95.4 19.6 reduce-scatter.6
